TPU v7x, 32 devices: a whole 2x2x4 slice. The times are simulated.
32 devices in a mesh: parts: 2 (over y), tmpl: 4 (over z), sta: 4 (over x, core).
Axes of the slice: x: 2, y: 2, z: 4, core: 2. Of those that a mesh axis runs over, the one named last changes fastest.
Arguments:
- data: float32 [64, 3, 1280], P(('parts', 'sta'), None, 'tmpl'), parts along dimension 0, as said below
- templates: bfloat16 [32, 3, 16, 256], P('sta', None, 'tmpl'), as said below
- starts: int32 [32, 3, 16], P('sta', None, 'tmpl'), may hold values from 0 to 512
Outputs:
- network: float32 [32, 512], P(('parts', 'tmpl'), 'sta'), parts along dimension 0
There are 2 independent parts, one for each index of `parts`. A program takes and returns all parts, laid end to end along the dimension named above; an argument that names none is the same for every part. Nothing has to cross between parts.
Inputs may be any that keep to these rules, and one draw needn't show every extreme that they name: `data`: finite samples. `templates`: finite samples.
All inputs are finite; a program needn't handle non-finite values.
Results may differ from a plain program's by a relative error of at most 0.0029.
Values sent between devices are 32-bit elements; how exact they have to be, the bound alone decides.
A program may use at most 64 MiB of HBM per device.

v0:
```python
import jax
import jax.numpy as jnp
from jax import lax
from jax.sharding import PartitionSpec as P

TLEN = 256
MAXSHIFT = 512
LAGS = 512
EPS = 1e-06


def window_energy(trace):
    extent = LAGS + MAXSHIFT
    squares = trace * trace
    running = jnp.concatenate([jnp.zeros_like(squares[:, :1]), jnp.cumsum(squares, axis=1)], axis=1)
    return running[:, TLEN : TLEN + extent] - running[:, :extent]


def take_window(row, offset):
    return lax.dynamic_slice_in_dim(row, offset, LAGS, 0)


def local_term(whole, templates, starts):
    extent = LAGS + MAXSHIFT
    stations, channels, samples = whole.shape
    per_group = templates.shape[2]
    groups = stations * channels
    lowered = whole.astype(jnp.bfloat16).reshape(1, groups, samples)
    kernel = templates.reshape(groups * per_group, 1, templates.shape[-1])
    raw = lax.conv_general_dilated(
        lowered,
        kernel,
        (1,),
        "VALID",
        dimension_numbers=("NCH", "OIH", "NCH"),
        feature_group_count=groups,
        preferred_element_type=jnp.float32,
    )[0]
    raw = raw[:, :extent]
    energy = window_energy(whole.reshape(groups, samples))
    energy_rows = jnp.repeat(energy, per_group, axis=0)
    tnorm = jnp.sum(jnp.square(templates.astype(jnp.float32)), axis=-1).reshape(-1)
    offsets = starts.reshape(-1)
    slicer = jax.vmap(take_window)
    aligned = slicer(raw, offsets)
    local = slicer(energy_rows, offsets)
    scale = TLEN * jnp.sqrt((tnorm[:, None] / TLEN + EPS) * (local / TLEN + EPS))
    return jnp.sum((aligned / scale).reshape(groups, per_group, LAGS), axis=0)


def shards(data, templates, starts):
    whole = lax.all_gather(data, "tmpl", axis=2, tiled=True)
    partial_value = local_term(whole, templates, starts)
    summed = lax.psum(partial_value, "sta")
    width = LAGS // lax.axis_size("sta")
    return lax.dynamic_slice_in_dim(summed, lax.axis_index("sta") * width, width, 1)


def solution(mesh):
    return jax.shard_map(
        shards,
        mesh=mesh,
        in_specs=(
            P(("parts", "sta"), None, "tmpl"),
            P("sta", None, "tmpl", None),
            P("sta", None, "tmpl"),
        ),
        out_specs=P(("parts", "tmpl"), "sta"),
        check_vma=False,
    )
```

profile of v0, /device:TPU:0, one launch (start us, length us, event | category | flops | bytes accessed | tf_op | source)
XLA Modules:
  0.0 490.5 jit_solution(16499657202032533554)
XLA Ops:
  1.0 47.9 %all_gather.3 = f32[8,3,1280]{0,1,2:T(4,128)S(1)} all-gather(f32[8,3,320]{0,1,2:T(4,128)S(1)} %copy.29), channel_id=1, replica_groups=mesh['parts'=2,'tmpl'=4,'sta'=4] {'tmpl'}, dimensions={2}, use_global_device_ids=true | all-gather | bytes 153600 | tf_op jit(solution)/shard_map/all_gather | solution.py:52
  49.9 6.8 %reduce-window.6 = f32[24,10,128]{2,1,0:T(8,128)S(1)} reduce-window(f32[24,10,128]{2,1,0:T(8,128)S(1)} %mul.25, f32[]{:T(128)} %constant.9.clone.1), window={size=1x1x128 pad=0_0x0_0x127_0}, to_apply=%region_1.2 | reduce-window | flops 3901440 | bytes 245764 | tf_op jit(solution)/shard_map/reduce-window
  58.0 197.6 %while.3 = (s32[]{:T(128)}, f32[96,1024]{1,0:T(8,128)S(1)}, s32[96,2]{0,1:T(2,128)S(1)}, f32[96,512]{1,0:T(8,128)S(1)}, s32[]{:T(128)}, /*index=5*/s32[]{:T(128)}) while((s32[]{:T(128)}, f32[96,1024]{1,0:T(8,128)S(1)}, s32[96,2]{0,1:T(2,128)S(1)}, f32[96,512]{1,0:T(8,128)S(1)}, s32[]{:T(128)}, /*index=5*/s32[]{:T(128)}) %tuple.38), condition=%wide.while_cond.1, body=%wide.while_body.1.sunk | while | flops 2 | bytes 8305 | solution.py:20
  75.2 1.3 dynamic-slice.15
  77.2 1.3 dynamic-slice.15
  79.3 1.3 dynamic-slice.15
  81.3 1.3 dynamic-slice.15
  83.4 1.3 dynamic-slice.15
  85.5 1.3 dynamic-slice.15
  87.5 1.3 dynamic-slice.15
  89.6 1.3 dynamic-slice.15
  91.6 1.3 dynamic-slice.15
  114.3 1.3 dynamic-slice.15
  116.3 1.3 dynamic-slice.15
  118.4 1.3 dynamic-slice.15
  120.5 1.3 dynamic-slice.15
  122.5 1.3 dynamic-slice.15
  124.6 1.3 dynamic-slice.15
  126.6 1.3 dynamic-slice.15
  128.7 1.3 dynamic-slice.15
  130.7 1.3 dynamic-slice.15
  153.4 1.3 dynamic-slice.15
  155.4 1.3 dynamic-slice.15
  157.5 1.3 dynamic-slice.15
  159.6 1.3 dynamic-slice.15
  161.6 1.3 dynamic-slice.15
  163.7 1.3 dynamic-slice.15
  165.7 1.3 dynamic-slice.15
  167.8 1.3 dynamic-slice.15
  169.9 1.3 dynamic-slice.15
  192.5 1.3 dynamic-slice.15
  194.6 1.3 dynamic-slice.15
  196.6 1.3 dynamic-slice.15
  198.7 1.3 dynamic-slice.15
  200.7 1.3 dynamic-slice.15
  202.8 1.3 dynamic-slice.15
  204.8 1.3 dynamic-slice.15
  206.9 1.3 dynamic-slice.15
  209.0 1.3 dynamic-slice.15
  231.6 1.3 dynamic-slice.15
  233.7 1.3 dynamic-slice.15
  235.7 1.3 dynamic-slice.15
  237.8 1.3 dynamic-slice.15
  239.8 1.3 dynamic-slice.15
  241.9 1.3 dynamic-slice.15
  256.5 28.5 %fusion.1 = f32[1,96,1025]{1,0,2:T(1,128)S(1)} fusion(bf16[1,24,1280]{1,0,2:T(2,128)(2,1)S(1)} %copy.33, s32[96]{0:T(128)S(1)} %copy-done.2, bf16[96,256]{0,1:T(8,128)(2,1)S(1)} %copy.32), kind=kOutput, calls=%fused_computation.4 | convolution fusion | flops 1210318848 | bytes 504576 | tf_op jit(solution)/shard_map/conv_general_dilated | solution.py:30
  285.8 197.6 %while.2 = (s32[]{:T(128)}, f32[96,1024]{1,0:T(8,128)S(1)}, s32[96,2]{0,1:T(2,128)S(1)}, f32[96,512]{1,0:T(8,128)S(1)}, s32[]{:T(128)}, /*index=5*/s32[]{:T(128)}) while((s32[]{:T(128)}, f32[96,1024]{1,0:T(8,128)S(1)}, s32[96,2]{0,1:T(2,128)S(1)}, f32[96,512]{1,0:T(8,128)S(1)}, s32[]{:T(128)}, /*index=5*/s32[]{:T(128)}) %tuple.41), condition=%wide.while_cond, body=%wide.while_body.sunk | while | flops 2 | bytes 8305 | solution.py:20
  484.1 5.8 %psum.7 = f32[4,512]{1,0:T(4,128)S(1)} all-reduce(f32[4,512]{1,0:T(4,128)S(1)} %fusion.5), channel_id=1, replica_groups=mesh['parts'=2,'tmpl'=4,'sta'=4] {'sta'}, use_global_device_ids=true, to_apply=%region_4.5 | all-reduce | flops 2048 | bytes 16384 | tf_op jit(solution)/shard_map/psum | solution.py:54
  (770 shorter events, 340.9 us)
Async XLA Ops:
  56.7 1.0 copy-start.1
  57.6 198.7 %copy-start = (bf16[8,3,4,256]{3,2,1,0:T(4,128)(2,1)S(1)}, bf16[8,3,4,256]{3,2,1,0:T(4,128)(2,1)}, u32[]{:S(2)}) copy-start(bf16[8,3,4,256]{3,2,1,0:T(4,128)(2,1)} %param.4) | copy-start | bytes 147460
  57.6 198.9 %copy-start.2 = (s32[96]{0:T(128)S(1)}, s32[96]{0:T(128)}, u32[]{:S(2)}) copy-start(s32[96]{0:T(128)} %constant.11.clone.1) | copy-start | bytes 1156
where the time goes:
time: 494 us; the launch traced here: 490 us
  local copies, waits for them, and re-layouts  396 us (80%)
  blocking collectives  53.7 us (11%)
  matrix products  28.5 us (6%)
  other arithmetic  7.52 us (2%)
    gather x768, local copies, waits for them, and re-layouts  391 us
    all_gather x1, blocking collectives, shards(): whole = lax.all_gather(data, 'tmpl', axis=2, tiled=True)  47.9 us
    conv_general_dilated x1, matrix products, local_term(): lax.conv_general_dilated(lowered, kernel, (1,), 'VALID', dimension_number...  28.5 us

commit v1 on v0

--- a/solution.py
+++ b/solution.py
@@ -1,3 +1,4 @@
+import functools
 import jax
 import jax.numpy as jnp
 from jax import lax
@@ -7,6 +8,25 @@
 MAXSHIFT = 512
 LAGS = 512
 EPS = 1e-06
+
+
+def number_zones(point, k_dim, along_axis):
+    axis_total = lax.psum(1, axis_name=along_axis)
+    it = 0
+    kept_rows = [point]
+    while it < axis_total - 1:
+        kept_rows.append(
+            lax.ppermute(
+                kept_rows[-1], along_axis, [(ii, (ii + 1) % axis_total) for ii in range(axis_total)]
+            )
+        )
+        it = it + 1
+    all_values = jnp.concatenate(kept_rows[::-1], k_dim)
+    high = jnp.roll(all_values, (lax.axis_index(along_axis) + 1) * point.shape[k_dim], k_dim)
+    return high
+
+
+update_chains_for = functools.partial(number_zones, k_dim=2, along_axis="tmpl")
 
 
 def window_energy(trace):
@@ -49,7 +69,7 @@
 
 
 def shards(data, templates, starts):
-    whole = lax.all_gather(data, "tmpl", axis=2, tiled=True)
+    whole = update_chains_for(data)
     partial_value = local_term(whole, templates, starts)
     summed = lax.psum(partial_value, "sta")
     width = LAGS // lax.axis_size("sta")

time: 494 us -> 464 us (0.939)
  blocking collectives: 53.7 us -> 5.77 us
  waiting for transfers between devices: 0 us -> 12.7 us
    all_gather x1 -> x0, blocking collectives: 47.9 us -> none  [shards(): whole = lax.all_gather(data, 'tmpl', axis=2, tiled=True)]
    ppermute x0 -> x3, waiting for transfers between devices: none -> 12.7 us  [number_zones(): lax.ppermute(kept_rows[-1], along_axis, [(ii, (ii + 1) % axis_total) for...]
  transfers between devices with their start and end apart: 0 -> 3, of which waited for: 0 -> 3; matrix products, arithmetic and copies ran while one was open for 0% -> 1% of each run, Pallas kernels for 0% -> 0%
where the time goes in v1:
time: 464 us; the launch traced here: 460 us
  local copies, waits for them, and re-layouts  397 us (86%)
  matrix products  28.5 us (6%)
  waiting for transfers between devices  12.7 us (3%)
  other arithmetic  8.38 us (2%)
  blocking collectives  5.77 us (1%)
  loops' own time  4.65 us (1%)
    gather x768, local copies, waits for them, and re-layouts  391 us
    conv_general_dilated x1, matrix products, local_term(): lax.conv_general_dilated(lowered, kernel, (1,), 'VALID', dimension_number...  28.5 us
    ppermute x3, waiting for transfers between devices, number_zones(): lax.ppermute(kept_rows[-1], along_axis, [(ii, (ii + 1) % axis_total) for...  12.7 us
  transfers between devices with their start and end apart: 3, of which 3 were waited for; matrix products, arithmetic and copies ran while one was open for 1% of the time, Pallas kernels for 0%

profile of v1, /device:TPU:0, one launch (start us, length us, event | category | flops | bytes accessed | tf_op | source)
XLA Modules:
  0.0 459.8 jit_solution(16977570191847198459)
XLA Ops:
  0.0 3.0 collective-permute-start
  4.9 2.3 collective-permute-done
  7.2 5.7 %collective-permute-done.1 = f32[8,3,320]{2,0,1:T(8,128)S(1)} collective-permute-done((f32[8,3,320]{2,0,1:T(8,128)S(1)}, f32[8,3,320]{2,0,1:T(8,128)S(1)}, u32[]{:S(2)}, u32[]{:S(2)}) %collective-permute-start.1) | collective-permute-done | bytes 30752 | tf_op jit(solution)/shard_map/ppermute | solution.py:19
  14.1 4.6 %collective-permute-done.2 = f32[8,3,320]{2,0,1:T(8,128)S(1)} collective-permute-done((f32[8,3,320]{2,0,1:T(8,128)S(1)}, f32[8,3,320]{2,0,1:T(8,128)S(1)}, u32[]{:S(2)}, u32[]{:S(2)}) %collective-permute-start.2) | collective-permute-done | bytes 30752 | tf_op jit(solution)/shard_map/ppermute | solution.py:19
  20.1 6.8 %reduce-window.6 = f32[24,10,128]{2,1,0:T(8,128)S(1)} reduce-window(f32[24,10,128]{2,1,0:T(8,128)S(1)} %mul.29, f32[]{:T(128)} %constant.52.clone.1), window={size=1x1x128 pad=0_0x0_0x127_0}, to_apply=%region_1.2 | reduce-window | flops 3901440 | bytes 245764 | tf_op jit(solution)/shard_map/reduce-window
  27.9 197.6 %while.3 = (s32[]{:T(128)}, f32[96,1024]{1,0:T(8,128)S(1)}, s32[96,2]{0,1:T(2,128)S(1)}, f32[96,512]{1,0:T(8,128)S(1)}, s32[]{:T(128)}, /*index=5*/s32[]{:T(128)}) while((s32[]{:T(128)}, f32[96,1024]{1,0:T(8,128)S(1)}, s32[96,2]{0,1:T(2,128)S(1)}, f32[96,512]{1,0:T(8,128)S(1)}, s32[]{:T(128)}, /*index=5*/s32[]{:T(128)}) %tuple.37), condition=%wide.while_cond.1, body=%wide.while_body.1.sunk | while | flops 2 | bytes 8305 | solution.py:40
  28.5 1.3 dynamic-slice.15
  30.6 1.3 dynamic-slice.15
  32.7 1.3 dynamic-slice.15
  34.7 1.3 dynamic-slice.15
  36.8 1.3 dynamic-slice.15
  38.8 1.3 dynamic-slice.15
  40.9 1.3 dynamic-slice.15
  43.0 1.3 dynamic-slice.15
  65.6 1.3 dynamic-slice.15
  67.7 1.3 dynamic-slice.15
  69.7 1.3 dynamic-slice.15
  71.8 1.3 dynamic-slice.15
  73.8 1.3 dynamic-slice.15
  75.9 1.3 dynamic-slice.15
  77.9 1.3 dynamic-slice.15
  80.0 1.3 dynamic-slice.15
  82.1 1.3 dynamic-slice.15
  104.7 1.3 dynamic-slice.15
  106.8 1.3 dynamic-slice.15
  108.8 1.3 dynamic-slice.15
  110.9 1.3 dynamic-slice.15
  112.9 1.3 dynamic-slice.15
  115.0 1.3 dynamic-slice.15
  117.1 1.3 dynamic-slice.15
  119.1 1.3 dynamic-slice.15
  121.2 1.3 dynamic-slice.15
  143.8 1.3 dynamic-slice.15
  145.9 1.3 dynamic-slice.15
  147.9 1.3 dynamic-slice.15
  150.0 1.3 dynamic-slice.15
  152.1 1.3 dynamic-slice.15
  154.1 1.3 dynamic-slice.15
  156.2 1.3 dynamic-slice.15
  158.2 1.3 dynamic-slice.15
  160.3 1.3 dynamic-slice.15
  182.9 1.3 dynamic-slice.15
  185.0 1.3 dynamic-slice.15
  187.0 1.3 dynamic-slice.15
  189.1 1.3 dynamic-slice.15
  226.2 28.5 %fusion.1 = f32[1,96,1025]{1,0,2:T(1,128)S(1)} fusion(bf16[1,24,1280]{1,0,2:T(2,128)(2,1)S(1)} %copy.30, s32[96]{0:T(128)S(1)} %copy-done, bf16[96,256]{0,1:T(8,128)(2,1)S(1)} %copy.29), kind=kOutput, calls=%fused_computation.4 | convolution fusion | flops 1210318848 | bytes 504576 | tf_op jit(solution)/shard_map/conv_general_dilated | solution.py:50
  255.6 197.6 %while.2 = (s32[]{:T(128)}, f32[96,1024]{1,0:T(8,128)S(1)}, s32[96,2]{0,1:T(2,128)S(1)}, f32[96,512]{1,0:T(8,128)S(1)}, s32[]{:T(128)}, /*index=5*/s32[]{:T(128)}) while((s32[]{:T(128)}, f32[96,1024]{1,0:T(8,128)S(1)}, s32[96,2]{0,1:T(2,128)S(1)}, f32[96,512]{1,0:T(8,128)S(1)}, s32[]{:T(128)}, /*index=5*/s32[]{:T(128)}) %tuple.40), condition=%wide.while_cond, body=%wide.while_body.sunk | while | flops 2 | bytes 8305 | solution.py:40
  453.5 5.8 %psum.7 = f32[4,512]{1,0:T(4,128)S(1)} all-reduce(f32[4,512]{1,0:T(4,128)S(1)} %fusion.5), channel_id=1, replica_groups=mesh['parts'=2,'tmpl'=4,'sta'=4] {'sta'}, use_global_device_ids=true, to_apply=%region_4.5 | all-reduce | flops 2048 | bytes 16384 | tf_op jit(solution)/shard_map/psum | solution.py:74
  (771 shorter events, 346.5 us)
Async XLA Ops:
  0.0 7.2 %collective-permute-start = (f32[8,3,320]{2,0,1:T(8,128)}, f32[8,3,320]{2,0,1:T(8,128)S(1)}, u32[]{:S(2)}, u32[]{:S(2)}) collective-permute-start(f32[8,3,320]{2,0,1:T(8,128)} %param.3), channel_id=1, source_target_pairs={{0,4},{4,8},{8,12},{12,0},{1,5},{5,9},{9,13},{13,1},{2,6},{6,10},{... | collective-permute-start | bytes 92168 | tf_op jit(solution)/shard_map/ppermute | solution.py:19
  7.2 5.8 %collective-permute-start.1 = (f32[8,3,320]{2,0,1:T(8,128)S(1)}, f32[8,3,320]{2,0,1:T(8,128)S(1)}, u32[]{:S(2)}, u32[]{:S(2)}) collective-permute-start(f32[8,3,320]{2,0,1:T(8,128)S(1)} %collective-permute-done), channel_id=1, source_target_pairs={{0,4},{4,8},{8,12},{12,0},{1,5},{5,9},{9,13},{13,1},{2,6},{6,10},{... | collective-permute-start | bytes 92168 | tf_op jit(solution)/shard_map/ppermute | solution.py:19
  13.0 5.8 %collective-permute-start.2 = (f32[8,3,320]{2,0,1:T(8,128)S(1)}, f32[8,3,320]{2,0,1:T(8,128)S(1)}, u32[]{:S(2)}, u32[]{:S(2)}) collective-permute-start(f32[8,3,320]{2,0,1:T(8,128)S(1)} %collective-permute-done.1), channel_id=1, source_target_pairs={{0,4},{4,8},{8,12},{12,0},{1,5},{5,9},{9,13},{13,1},{2,6},{6,10},{... | collective-permute-start | bytes 92168 | tf_op jit(solution)/shard_map/ppermute | solution.py:19
  225.5 0.7 copy-start
